TPU v7x, 32 devices: a whole 2x2x4 slice. The times are simulated.
32 devices in a mesh: agg: 8 (over z, x), col: 4 (over y, core).
Axes of the slice: x: 2, y: 2, z: 4, core: 2. Of those that a mesh axis runs over, the one named last changes fastest.
Arguments:
- fine_tiles: bfloat16 [128, 4, 192, 192], P('agg', 'col')
- fine_cols: int32 [128, 4], P('agg', 'col'), may hold values from 0 to 127, as said below
- agg_of: int32 [128], P('agg'), may hold values from 0 to 31, as said below
- prolong: bfloat16 [128, 192, 192], P('agg'), may hold values from -0.21875 to 0.21875
- coarse_cols: int32 [32, 4], P('agg'), may hold values from 0 to 31, as said below
Outputs:
- coarse_tiles: float32 [32, 4, 192, 192], P('agg', 'col')
- factor_tiles: float32 [32, 4, 192, 192], P('agg', 'col')
Inputs may be any that keep to these rules, and one draw needn't show every extreme that they name: Fine block row i belongs to an aggregate of its own index of agg: i // 16 * 4 <= agg_of[i] < i // 16 * 4 + 4; every aggregate has at least one fine row. `coarse_cols`: slot 0 of aggregate row c is c itself; the other slots are distinct aggregates c + o with 1 <= |o| <= 4. `fine_cols`: slot 0 of fine row i is i; for slots 1 and above the aggregate of the named fine row is one of the slots 1 and above of row agg_of[i] of coarse_cols.
All inputs are finite; a program needn't handle non-finite values.
Results may differ from a plain program's by a relative error of at most 0.0055.
Values may be sent and summed in bfloat16 or wider, within the bound.
A program may use at most 128 MiB of HBM per device.

v0:
```python
import functools

import jax
import jax.numpy as jnp
from jax import lax
from jax.experimental import pallas as pl
from jax.experimental.pallas import tpu as pltpu
from jax.sharding import PartitionSpec as P

SWEEPS = 2
MESH = pl.DeviceIdType.MESH
BF = jnp.bfloat16
F32 = jnp.float32


def pack(tile, dtype):
    width = tile.shape[-1]
    lanes = 2 * width // 3
    half = width // 2
    rest = tile[:, lanes:]
    return tile[:, :lanes].astype(dtype), jnp.concatenate([rest[:half], rest[half:]], axis=1).astype(dtype)


def put(ref, index, tile):
    left, rest = pack(tile, ref.dtype)
    width = tile.shape[-1]
    ref[index, 0:width] = left
    ref[index, width:] = rest


def unpack(tile, width):
    half = width // 2
    rest = tile[width:]
    fold = width - tile.shape[-1]
    right = jnp.concatenate([rest[:, :fold], rest[:, fold:]], axis=0)
    return jnp.concatenate([tile[:width], right], axis=1)


def kernel(
    dims, ints, fine_hbm, prolong_hbm, coarse_out, factor_out,
    fine, own_prolong, near, seg, rs_out, rs_in, ext_a, ext_b, tab_v, tab, cls, order, table,
    in_sem, t_sem, t_send, t_recv,
    h_send, h_recv, r_send, r_recv, a_send, a_recv, b_send, b_recv,
):
    groups, peers, rows, crows, slots, width = dims
    a = lax.axis_index("agg")
    c = lax.axis_index("col")
    c1 = c + 1 - 2 * (c % 2)
    c2 = (c + 2) % peers
    c3 = c2 + 1 - 2 * (c2 % 2)
    has_prev = a > 0
    has_next = a < groups - 1
    share = rows // peers
    o_coarse = rows
    o_fine = o_coarse + crows * slots
    o_last = 0
    o_some = o_last + crows * slots
    o_spot = o_some + crows * slots
    o_flag = o_spot + crows * slots
    o_diag = o_flag + crows * slots

    take_share = pltpu.make_async_copy(
        prolong_hbm.at[pl.ds(c * share, share)],
        own_prolong.at[pl.ds(c * share, share)], in_sem.at[0],
    )
    take_share.start()

    def take_other(j):
        part_of = (c + j) % peers
        return pltpu.make_async_copy(
            prolong_hbm.at[pl.ds(part_of * share, share)],
            own_prolong.at[pl.ds(part_of * share, share)], in_sem.at[j],
        )

    for j in range(1, peers):
        take_other(j).start()
    take_fine = pltpu.make_async_copy(fine_hbm, fine, in_sem.at[peers])
    take_fine.start()

    barrier = pltpu.get_barrier_semaphore()
    for other in (c1, c2, c3):
        pl.semaphore_signal(barrier, inc=1, device_id=(a, other), device_id_type=MESH)

    @pl.when(has_prev)
    def _():
        pl.semaphore_signal(barrier, inc=1, device_id=(a - 1, c), device_id_type=MESH)

    @pl.when(has_next)
    def _():
        pl.semaphore_signal(barrier, inc=1, device_id=(a + 1, c), device_id_type=MESH)

    def remote(src, dst, send, recv, device):
        return pltpu.make_async_remote_copy(
            src_ref=src, dst_ref=dst, send_sem=send, recv_sem=recv,
            device_id=device, device_id_type=MESH,
        )

    def pack_own(first):
        def body(k, carry):
            put(near, rows + first + k, own_prolong[first + k].astype(F32))
            return carry
        lax.fori_loop(0, share, body, 0)

    take_share.wait()
    pack_own(c * share)

    @pl.when(has_prev & has_next)
    def _():
        pl.semaphore_wait(barrier, 5)

    @pl.when(jnp.logical_not(has_prev & has_next))
    def _():
        pl.semaphore_wait(barrier, 4)

    def ints_to(g, device):
        return remote(ints, tab_v.at[2 - 2 * g], t_send.at[g], t_recv.at[1 - g], device)

    def push(g, k, device):
        src = near.at[pl.ds(rows + c * share + k, 1)]
        dst = near.at[pl.ds((2 - g * 2) * rows + c * share + k, 1)]
        return remote(src, dst, h_send.at[1 - g, 0, k], h_recv.at[1 - g, 0, k], device)

    def push_all(act):
        @pl.when(has_next)
        def _():
            act(ints_to(1, (a + 1, c)))

        @pl.when(has_prev)
        def _():
            act(ints_to(0, (a - 1, c)))

        for k in range(share):
            @pl.when(has_next)
            def _():
                act(push(1, k, (a + 1, c)))

            @pl.when(has_prev)
            def _():
                act(push(0, k, (a - 1, c)))

    push_all(lambda copy: copy.start())
    for j in range(1, peers):
        take_other(j).wait()
        pack_own(((c + j) % peers) * share)

    def spreader(buf, at, send, recv):
        def hop(g, kind, who, k, device):
            view = buf.at[pl.ds(at(g, who) + k, 1)]
            return remote(view, view, send.at[g, kind, k], recv.at[g, kind, k], device)

        class Steps:
            def share(g, k):
                hop(g, 2, c, k, (a, c2)).start()
                hop(g, 1, c, k, (a, c1)).start()

            def first(g, k):
                hop(g, 0, c, k, (a, c1)).wait_recv()
                Steps.share(g, k)

            def second(g, k):
                hop(g, 2, c2, k, (a, c2)).wait_recv()
                hop(g, 3, c2, k, (a, c1)).start()

            def third(g, k):
                hop(g, 1, c1, k, (a, c1)).wait_recv()
                hop(g, 3, c3, k, (a, c1)).wait_recv()

            def done(g, k):
                hop(g, 2, c, k, (a, c2)).wait_send()
                hop(g, 1, c, k, (a, c1)).wait_send()
                hop(g, 3, c2, k, (a, c1)).wait_send()

        return Steps

    halo = spreader(near, lambda g, who: g * 2 * rows + who * share, h_send, h_recv)
    sides = ((0, has_prev), (1, has_next))

    def each_side(step):
        for k in range(share):
            for g, condition in sides:
                pl.when(condition)(functools.partial(step, g, k))

    def to_scalar(g):
        return pltpu.make_async_copy(tab_v.at[g], tab.at[g], t_sem.at[g])

    own_ints = pltpu.make_async_copy(ints, tab.at[1], t_sem.at[1])
    own_ints.start()

    each_side(halo.first)
    own_ints.wait()

    @pl.when(has_prev)
    def _():
        ints_to(1, (a - 1, c)).wait_recv()
        to_scalar(0).start()
        to_scalar(0).wait()

    @pl.when(has_next)
    def _():
        ints_to(0, (a + 1, c)).wait_recv()
        to_scalar(2).start()
        to_scalar(2).wait()

    row_base = a * crows
    ext_base = row_base - crows

    def mine(k):
        return tab[1, 0, k]

    def place_of(i):
        return mine(o_fine + i) - (a - 1) * rows

    def classify(i, carry):
        place = jnp.clip(place_of(i), 0, 3 * rows - 1)
        target = tab[place // rows, 0, place % rows]
        r = jnp.clip(mine(i) - row_base, 0, crows - 1)
        q = 0
        for s in range(1, slots):
            q = jnp.where(mine(o_coarse + r * slots + s) == target, s, q)
        cls[i] = (r * slots + q) * rows + i
        return carry

    lax.fori_loop(0, rows, classify, 0)

    def rank(i, carry):
        key = cls[i]
        below = 0
        for j in range(rows):
            below = below + jnp.where(cls[j] < key, 1, 0)
        order[rows + i] = below
        return carry

    lax.fori_loop(0, rows, rank, 0)

    def place_key(k, carry):
        key = 0
        for i in range(rows):
            key = key + jnp.where(order[rows + i] == k, cls[i], 0)
        order[k] = key
        return carry

    lax.fori_loop(0, rows, place_key, 0)

    def ends(s, carry):
        upto = 0
        some = 0
        for i in range(rows):
            own_class = cls[i] // rows
            upto = upto + jnp.where(own_class <= s, 1, 0)
            some = jnp.where(own_class == s, 1, some)
        table[o_last + s] = jnp.maximum(upto - 1, 0)
        table[o_some + s] = some
        return carry

    lax.fori_loop(0, crows * slots, ends, 0)

    def ties(r, carry):
        row = row_base + r
        column = mine(o_coarse + r * slots + c)
        lowest = jnp.minimum(row, column)
        for m in range(1, slots):
            prior = mine(o_coarse + r * slots + m)
            k = jnp.clip(prior - ext_base, 0, 2 * crows - 1)
            g = k // crows
            slot = 0
            found = 0
            for n in range(slots):
                same = tab[g, 0, o_coarse + (k % crows) * slots + n] == column
                slot = jnp.where(same, n, slot)
                found = jnp.where(same, 1, found)
            found = jnp.where(prior < lowest, found, 0)
            spot = (g * slots + slot) * crows + k % crows
            table[o_spot + r * slots + m] = jnp.where(found == 1, spot, slots * crows)
            table[o_flag + r * slots + m] = found
        k = jnp.clip(column - ext_base, 0, 2 * crows - 1)
        table[o_diag + r] = jnp.where(
            column < row, (k // crows) * slots * crows + k % crows, slots * crows + r
        )
        return carry

    lax.fori_loop(0, crows, ties, 0)

    each_side(halo.second)
    take_fine.wait()
    each_side(halo.third)

    def lift(k, total):
        key = order[k]
        i = key % rows
        earlier = order[jnp.maximum(k - 1, 0)]
        goes_on = jnp.where(earlier // rows == key // rows, 1, 0)
        place = jnp.clip(place_of(i), 0, 3 * rows - 1)
        carried = jnp.dot(
            fine[i], unpack(near[place], width), preferred_element_type=F32
        ).astype(BF)
        lifted = lax.dot_general(
            own_prolong[i], carried, (((0,), (0,)), ((), ())), preferred_element_type=F32
        )
        total = lifted + total * goes_on.astype(F32)
        seg[k] = total
        return total

    lax.fori_loop(0, rows, lift, jnp.zeros((width, width), F32))

    def part(r, q):
        s = r * slots + q
        return seg[table[o_last + s]] * table[o_some + s].astype(F32)

    others = slots - 1

    def partner(j):
        return 1 + (c - 1 + j) % others

    def give(j, r):
        return remote(
            rs_out.at[pl.ds(j * crows + r, 1)], rs_in.at[pl.ds((others - j) * crows + r, 1)],
            r_send.at[j, r], r_recv.at[others - j, r], (a, partner(j)),
        )

    @pl.when(c > 0)
    def _():
        for r in range(crows):
            for j in range(1, others):
                put(rs_out, j * crows + r, part(r, partner(j)))
                give(j, r).start()

    own_at = (slots + c) * crows
    exts = (ext_a, ext_b)
    gather = [
        spreader(ext, lambda g, who: (g * slots + who) * crows, send, recv)
        for ext, send, recv in ((ext_a, a_send, a_recv), (ext_b, b_send, b_recv))
    ]

    def onward(step, r):
        send, recv = ((a_send, a_recv), (b_send, b_recv))[step]
        ext = exts[step]
        return remote(
            ext.at[pl.ds(own_at + r, 1)], ext.at[pl.ds(c * crows + r, 1)],
            send.at[0, 0, r], recv.at[0, 0, r], (a + 1, c),
        )

    def send_row(step, r):
        gather[step].share(1, r)

        @pl.when(has_next)
        def _():
            onward(step, r).start()

    for r in range(crows):
        @pl.when(c == 0)
        def _():
            value = part(r, 0)
            coarse_out[r, 0] = value
            put(ext_a, own_at + r, value)

        @pl.when(c > 0)
        def _():
            value = part(r, c)
            for j in range(1, others):
                give(others - j, r).wait_recv()
                value = value + unpack(rs_in[j * crows + r].astype(F32), width)
            coarse_out[r, 0] = value
            put(ext_a, own_at + r, value)

        send_row(0, r)

    ids_r = lax.broadcasted_iota(jnp.int32, (width, width), 0)
    ids_c = lax.broadcasted_iota(jnp.int32, (width, width), 1)
    above = (ids_c > ids_r).astype(F32)
    below = (ids_c < ids_r).astype(F32)
    on = ids_c == ids_r

    for step in range(SWEEPS):
        ext = exts[step]
        old = coarse_out if step == 0 else factor_out
        steps = gather[step]
        for k in range(crows):
            pl.when(has_prev)(functools.partial(steps.first, 0, k))
            steps.second(1, k)
        for k in range(crows):
            pl.when(has_prev)(functools.partial(steps.second, 0, k))
        for k in range(crows):
            steps.third(1, k)
            pl.when(has_prev)(functools.partial(steps.third, 0, k))

        def relax(r, carry, ext=ext, old=old, step=step):
            row = row_base + r
            column = mine(o_coarse + r * slots + c)
            value = coarse_out[r, 0]
            for m in range(1, slots):
                s = r * slots + m
                left = unpack(ext[(slots + m) * crows + r], width)
                right = unpack(ext[table[o_spot + s]], width)
                value = value - table[o_flag + s].astype(F32) * jnp.dot(
                    left, right, preferred_element_type=F32
                )
            low = jnp.full((width, width), jnp.where(row > column, 1, 0)) == 1
            up = jnp.full((width, width), jnp.where(row < column, 1, 0)) == 1
            before = old[r, 0]
            own_diag = unpack(ext[slots * crows + r].astype(F32), width)
            their_diag = unpack(ext[table[o_diag + r]].astype(F32), width)
            left = jnp.where(low, before, own_diag * below)
            right = jnp.where(up, before, their_diag * above)
            value = value - jnp.dot(
                left.astype(BF), right.astype(BF), preferred_element_type=F32
            )
            pivots = jnp.maximum(
                jnp.sum(jnp.where(on, their_diag, 0.0), axis=0, keepdims=True), 1.0
            )
            scaled = low | (jnp.logical_not(up) & (ids_c < ids_r))
            value = jnp.where(scaled, value / pivots, value)
            factor_out[r, 0] = value
            if step < SWEEPS - 1:
                put(exts[step + 1], own_at + r, value)
                send_row(step + 1, r)
            return carry

        lax.fori_loop(0, crows, relax, 0)

    push_all(lambda copy: copy.wait_send())
    each_side(halo.done)

    @pl.when(c > 0)
    def _():
        for r in range(crows):
            for j in range(1, others):
                give(j, r).wait_send()

    for step in range(SWEEPS):
        for k in range(crows):
            gather[step].done(1, k)

            @pl.when(has_prev)
            def _():
                gather[step].done(0, k)

            @pl.when(has_next)
            def _():
                onward(step, k).wait_send()


def on_device(groups, peers, fine_tiles, fine_cols, agg_of, prolong, coarse_cols):
    rows, width = prolong.shape[0], prolong.shape[-1]
    crows, slots = coarse_cols.shape
    assert SWEEPS == 2 and slots == peers == 4 and fine_tiles.shape[1] == 1
    ints = jnp.concatenate([agg_of, coarse_cols.reshape(-1), fine_cols.reshape(-1)])
    room = -(-ints.shape[0] // 128) * 128
    ints = jnp.pad(ints, (0, room - ints.shape[0])).reshape(1, room)
    share = rows // peers
    dma = pltpu.SemaphoreType.DMA
    tile = (width, width)
    packed = (width + width // 2, 2 * width // 3)
    out = jax.ShapeDtypeStruct((crows, 1) + tile, F32)
    vmem = pl.BlockSpec(memory_space=pltpu.VMEM)
    anywhere = pl.BlockSpec(memory_space=pl.ANY)
    return pl.pallas_call(
        functools.partial(kernel, (groups, peers, rows, crows, slots, width)),
        out_shape=(out, out),
        in_specs=[vmem, anywhere, anywhere],
        out_specs=(vmem, vmem),
        scratch_shapes=[
            pltpu.VMEM((rows,) + tile, BF),
            pltpu.VMEM((rows,) + tile, BF),
            pltpu.VMEM((3 * rows,) + packed, BF),
            pltpu.VMEM((rows,) + tile, F32),
            pltpu.VMEM((slots * crows,) + packed, BF),
            pltpu.VMEM((slots * crows,) + packed, BF),
            pltpu.VMEM((2 * slots * crows,) + packed, BF),
            pltpu.VMEM((2 * slots * crows,) + packed, BF),
            pltpu.VMEM((3, 1, room), jnp.int32),
            pltpu.SMEM((3, 1, room), jnp.int32),
            pltpu.SMEM((rows,), jnp.int32),
            pltpu.SMEM((2 * rows,), jnp.int32),
            pltpu.SMEM((4 * crows * slots + crows,), jnp.int32),
            dma((peers + 1,)), dma((3,)), dma((2,)), dma((2,)),
            dma((2, 4, share)), dma((2, 4, share)),
            dma((slots, crows)), dma((slots, crows)),
            dma((2, 4, crows)), dma((2, 4, crows)),
            dma((2, 4, crows)), dma((2, 4, crows)),
        ],
        compiler_params=pltpu.CompilerParams(
            collective_id=0, has_side_effects=True, vmem_limit_bytes=56 * 1024 * 1024
        ),
    )(ints, fine_tiles.reshape((rows,) + tile), prolong)


def solution(mesh):
    in_specs = (
        P("agg", "col", None, None),
        P("agg", "col"),
        P("agg"),
        P("agg", None, None),
        P("agg", None),
    )
    out_specs = (P("agg", "col", None, None), P("agg", "col", None, None))
    return jax.shard_map(
        functools.partial(on_device, mesh.shape["agg"], mesh.shape["col"]),
        mesh=mesh, in_specs=in_specs, out_specs=out_specs, check_vma=False,
    )
```

profile of v0, /device:TPU:29, one launch (start us, length us, event | category | flops | bytes accessed | tf_op | source)
XLA Modules:
  0.0 82.6 jit_solution(1313844363823295021)
XLA Ops:
  0.6 0.8 reshape.16
  1.4 0.7 pad_add_fusion
  2.1 0.5 pad_bitcast_fusion.ints
  2.7 76.9 %shard_map.68 = (f32[4,1,192,192]{3,2,1,0:T(8,128)}, f32[4,1,192,192]{3,2,1,0:T(8,128)}) custom-call(s32[1,128]{1,0:T(1,128)} %pad_bitcast_fusion.ints, bf16[16,192,192]{2,1,0:T(8,128)(2,1)} %bitcast.4, bf16[16,192,192]{2,1,0:T(8,128)(2,1)} %prolong_hbm.1), custom_call_target="tpu_custom_call" | custom-call | tf_op jit(solution)/shard_map/pallas_call | solution.py:456
  79.5 0.0 copy-start
  79.5 2.1 %copy.9 = f32[4,1,192,192]{3,2,1,0:T(8,128)} copy(f32[4,1,192,192]{3,2,1,0:T(8,128)} %get-tuple-element.4) | data formatting | bytes 1179648
  81.7 0.0 copy-done
  81.7 0.9 %copy.10 = f32[4,1,192,192]{3,2,1,0:T(8,128)} copy(f32[4,1,192,192]{3,2,1,0:T(8,128)S(1)} %copy-done) | data formatting | bytes 1179648
Async XLA Ops:
  79.5 2.1 %copy-start = (f32[4,1,192,192]{3,2,1,0:T(8,128)S(1)}, f32[4,1,192,192]{3,2,1,0:T(8,128)}, u32[]{:S(2)}) copy-start(f32[4,1,192,192]{3,2,1,0:T(8,128)} %get-tuple-element.5) | copy-start | bytes 1769476
where the time goes:
time: 82.8 us; the launch traced here: 82.6 us
  Pallas kernels  76.9 us (93%)
  local copies, waits for them, and re-layouts  4.3 us (5%)
    pallas_call x1, Pallas kernels, on_device(): pl.pallas_call(functools.partial(kernel, (groups, peers, rows, crows, slo...  76.9 us
    unnamed x4, local copies, waits for them, and re-layouts  3.02 us

commit v1 on v0

--- a/solution.py
+++ b/solution.py
@@ -38,7 +38,7 @@
 
 def kernel(
     dims, ints, fine_hbm, prolong_hbm, coarse_out, factor_out,
-    fine, own_prolong, near, seg, rs_out, rs_in, ext_a, ext_b, tab_v, tab, cls, order, table,
+    fine, own_prolong, turned, near, seg, rs_out, rs_in, ext_a, ext_b, tab_v, tab, cls, order, table,
     in_sem, t_sem, t_send, t_recv,
     h_send, h_recv, r_send, r_recv, a_send, a_recv, b_send, b_recv,
 ):
@@ -50,7 +50,15 @@
     c3 = c2 + 1 - 2 * (c2 % 2)
     has_prev = a > 0
     has_next = a < groups - 1
-    share = rows // peers
+    parity = a % 2
+    partner_agg = a + 1 - 2 * parity
+    relay_to = a + 2 - 4 * parity
+    relay_from = a - 2 + 4 * parity
+    can_relay = (relay_to >= 0) & (relay_to < groups)
+    has_other = (relay_from >= 0) & (relay_from < groups)
+    alone = rows // (2 * peers)
+    both = rows // 4
+    direct = alone + both
     o_coarse = rows
     o_fine = o_coarse + crows * slots
     o_last = 0
@@ -59,22 +67,19 @@
     o_flag = o_spot + crows * slots
     o_diag = o_flag + crows * slots
 
-    take_share = pltpu.make_async_copy(
-        prolong_hbm.at[pl.ds(c * share, share)],
-        own_prolong.at[pl.ds(c * share, share)], in_sem.at[0],
-    )
-    take_share.start()
-
-    def take_other(j):
-        part_of = (c + j) % peers
+    blocks = [(c * alone, alone), (peers * alone + (c % 2) * both, both)]
+    blocks += [(other * alone, alone) for other in (c1, c2, c3)]
+    blocks += [(peers * alone + (c1 % 2) * both, both)]
+
+    def take(j):
+        start, size = blocks[j]
         return pltpu.make_async_copy(
-            prolong_hbm.at[pl.ds(part_of * share, share)],
-            own_prolong.at[pl.ds(part_of * share, share)], in_sem.at[j],
+            prolong_hbm.at[pl.ds(start, size)], own_prolong.at[pl.ds(start, size)], in_sem.at[j]
         )
 
-    for j in range(1, peers):
-        take_other(j).start()
-    take_fine = pltpu.make_async_copy(fine_hbm, fine, in_sem.at[peers])
+    for j in range(len(blocks)):
+        take(j).start()
+    take_fine = pltpu.make_async_copy(fine_hbm, fine, in_sem.at[6])
     take_fine.start()
 
     barrier = pltpu.get_barrier_semaphore()
@@ -88,6 +93,14 @@
     @pl.when(has_next)
     def _():
         pl.semaphore_signal(barrier, inc=1, device_id=(a + 1, c), device_id_type=MESH)
+
+    @pl.when(can_relay)
+    def _():
+        pl.semaphore_signal(barrier, inc=1, device_id=(relay_to, c), device_id_type=MESH)
+
+    @pl.when(has_other)
+    def _():
+        pl.semaphore_signal(barrier, inc=1, device_id=(relay_from, c), device_id_type=MESH)
 
     def remote(src, dst, send, recv, device):
         return pltpu.make_async_remote_copy(
@@ -95,32 +108,86 @@
             device_id=device, device_id_type=MESH,
         )
 
-    def pack_own(first):
+    def pack_own(j):
+        start, size = blocks[j]
+
         def body(k, carry):
-            put(near, rows + first + k, own_prolong[first + k].astype(F32))
+            put(near, rows + start + k, own_prolong[start + k].astype(F32))
             return carry
-        lax.fori_loop(0, share, body, 0)
-
-    take_share.wait()
-    pack_own(c * share)
-
-    @pl.when(has_prev & has_next)
+        lax.fori_loop(0, size, body, 0)
+
+    for j in range(2):
+        take(j).wait()
+        pack_own(j)
+
+    @pl.when((a > 1) & (a < groups - 2))
+    def _():
+        pl.semaphore_wait(barrier, 7)
+
+    @pl.when((a == 1) | (a == groups - 2))
+    def _():
+        pl.semaphore_wait(barrier, 6)
+
+    @pl.when((a == 0) | (a == groups - 1))
     def _():
         pl.semaphore_wait(barrier, 5)
-
-    @pl.when(jnp.logical_not(has_prev & has_next))
-    def _():
-        pl.semaphore_wait(barrier, 4)
 
     def ints_to(g, device):
         return remote(ints, tab_v.at[2 - 2 * g], t_send.at[g], t_recv.at[1 - g], device)
 
-    def push(g, k, device):
-        src = near.at[pl.ds(rows + c * share + k, 1)]
-        dst = near.at[pl.ds((2 - g * 2) * rows + c * share + k, 1)]
-        return remote(src, dst, h_send.at[1 - g, 0, k], h_recv.at[1 - g, 0, k], device)
-
-    def push_all(act):
+    def tile_of(who, k):
+        if k < alone:
+            return who * alone + k
+        return peers * alone + (who % 2) * both + k - alone
+
+    def block_at(side):
+        return ((1 - parity) if side == 0 else parity) * 2 * rows
+
+    def push(k):
+        src = near.at[pl.ds(rows + tile_of(c, k), 1)]
+        dst = near.at[pl.ds(parity * 2 * rows + tile_of(c, k), 1)]
+        return remote(src, dst, h_send.at[0, 0, k], h_recv.at[0, 0, k], (partner_agg, c))
+
+    def relay(k):
+        src = near.at[pl.ds(block_at(0) + tile_of(c, k), 1)]
+        dst = near.at[pl.ds(parity * 2 * rows + tile_of(c, k), 1)]
+        return remote(src, dst, h_send.at[1, 0, k], h_recv.at[1, 0, k], (relay_to, c))
+
+    def pass_on(side, kind, who, k, device):
+        view = near.at[pl.ds(block_at(side) + tile_of(who, k), 1)]
+        return remote(view, view, h_send.at[side, kind, k], h_recv.at[side, kind, k], device)
+
+    def arrived(side, k):
+        pass_on(side, 0, c, k, (a, c1)).wait_recv()
+        if side == 0:
+            @pl.when(can_relay)
+            def _():
+                relay(k).start()
+        if k < alone:
+            pass_on(side, 2, c, k, (a, c2)).start()
+        pass_on(side, 1, c, k, (a, c1)).start()
+
+    def crossed(side, k):
+        pass_on(side, 2, c2, k, (a, c2)).wait_recv()
+        pass_on(side, 3, c2, k, (a, c1)).start()
+
+    def complete(side):
+        for k in range(direct):
+            pass_on(side, 1, c1, k, (a, c1)).wait_recv()
+            if k < alone:
+                pass_on(side, 3, c3, k, (a, c1)).wait_recv()
+
+    def left(side):
+        for k in range(direct):
+            pass_on(side, 1, c, k, (a, c1)).wait_send()
+            if k < alone:
+                pass_on(side, 2, c, k, (a, c2)).wait_send()
+                pass_on(side, 3, c2, k, (a, c1)).wait_send()
+
+    def other_side(step, *args):
+        pl.when(has_other)(functools.partial(step, 1, *args))
+
+    def ints_all(act):
         @pl.when(has_next)
         def _():
             act(ints_to(1, (a + 1, c)))
@@ -129,19 +196,14 @@
         def _():
             act(ints_to(0, (a - 1, c)))
 
-        for k in range(share):
-            @pl.when(has_next)
-            def _():
-                act(push(1, k, (a + 1, c)))
-
-            @pl.when(has_prev)
-            def _():
-                act(push(0, k, (a - 1, c)))
-
-    push_all(lambda copy: copy.start())
-    for j in range(1, peers):
-        take_other(j).wait()
-        pack_own(((c + j) % peers) * share)
+    for k in range(direct):
+        push(k).start()
+    ints_all(lambda copy: copy.start())
+    for j in range(2, len(blocks)):
+        take(j).wait()
+        pack_own(j)
+
+    relayed = crows // 2
 
     def spreader(buf, at, send, recv):
         def hop(g, kind, who, k, device):
@@ -150,15 +212,26 @@
 
         class Steps:
             def share(g, k):
-                hop(g, 2, c, k, (a, c2)).start()
+                if g == 1 or k >= relayed:
+                    hop(g, 2, c, k, (a, c2)).start()
                 hop(g, 1, c, k, (a, c1)).start()
 
             def first(g, k):
                 hop(g, 0, c, k, (a, c1)).wait_recv()
                 Steps.share(g, k)
 
+            def beyond(k):
+                src = buf.at[pl.ds(at(1, c2) + k, 1)]
+                dst = buf.at[pl.ds(at(0, c2) + k, 1)]
+                return remote(src, dst, send.at[0, 4, k], recv.at[0, 4, k], (a + 1, c))
+
             def second(g, k):
-                hop(g, 2, c2, k, (a, c2)).wait_recv()
+                direct_row = g == 0 and k < relayed
+                hop(g, 4 if direct_row else 2, c2, k, (a, c2)).wait_recv()
+                if g == 1 and k < relayed:
+                    @pl.when(has_next)
+                    def _():
+                        Steps.beyond(k).start()
                 hop(g, 3, c2, k, (a, c1)).start()
 
             def third(g, k):
@@ -166,27 +239,31 @@
                 hop(g, 3, c3, k, (a, c1)).wait_recv()
 
             def done(g, k):
-                hop(g, 2, c, k, (a, c2)).wait_send()
+                if g == 1 or k >= relayed:
+                    hop(g, 2, c, k, (a, c2)).wait_send()
                 hop(g, 1, c, k, (a, c1)).wait_send()
                 hop(g, 3, c2, k, (a, c1)).wait_send()
 
         return Steps
 
-    halo = spreader(near, lambda g, who: g * 2 * rows + who * share, h_send, h_recv)
-    sides = ((0, has_prev), (1, has_next))
-
-    def each_side(step):
-        for k in range(share):
-            for g, condition in sides:
-                pl.when(condition)(functools.partial(step, g, k))
-
     def to_scalar(g):
         return pltpu.make_async_copy(tab_v.at[g], tab.at[g], t_sem.at[g])
 
     own_ints = pltpu.make_async_copy(ints, tab.at[1], t_sem.at[1])
     own_ints.start()
 
-    each_side(halo.first)
+    lag = 2
+    for k in range(direct + lag):
+        if k < direct:
+            arrived(0, k)
+        if k >= lag:
+            other_side(arrived, k - lag)
+
+    def turn(i, carry):
+        turned[i] = own_prolong[i].astype(F32).T.astype(BF)
+        return carry
+
+    lax.fori_loop(0, rows, turn, 0)
     own_ints.wait()
 
     @pl.when(has_prev)
@@ -280,9 +357,13 @@
 
     lax.fori_loop(0, crows, ties, 0)
 
-    each_side(halo.second)
+    for k in range(alone):
+        crossed(0, k)
+    for k in range(alone):
+        other_side(crossed, k)
     take_fine.wait()
-    each_side(halo.third)
+    complete(0)
+    other_side(complete)
 
     def lift(k, total):
         key = order[k]
@@ -293,14 +374,12 @@
         carried = jnp.dot(
             fine[i], unpack(near[place], width), preferred_element_type=F32
         ).astype(BF)
-        lifted = lax.dot_general(
-            own_prolong[i], carried, (((0,), (0,)), ((), ())), preferred_element_type=F32
-        )
+        lifted = jnp.dot(turned[i], carried, preferred_element_type=F32)
         total = lifted + total * goes_on.astype(F32)
         seg[k] = total
         return total
 
-    lax.fori_loop(0, rows, lift, jnp.zeros((width, width), F32))
+    lax.fori_loop(0, rows, lift, jnp.zeros((width, width), F32), unroll=4)
 
     def part(r, q):
         s = r * slots + q
@@ -375,8 +454,8 @@
         old = coarse_out if step == 0 else factor_out
         steps = gather[step]
         for k in range(crows):
+            steps.second(1, k)
             pl.when(has_prev)(functools.partial(steps.first, 0, k))
-            steps.second(1, k)
         for k in range(crows):
             pl.when(has_prev)(functools.partial(steps.second, 0, k))
         for k in range(crows):
@@ -417,8 +496,17 @@
 
         lax.fori_loop(0, crows, relax, 0)
 
-    push_all(lambda copy: copy.wait_send())
-    each_side(halo.done)
+    ints_all(lambda copy: copy.wait_send())
+    for k in range(direct):
+        push(k).wait_send()
+
+    @pl.when(can_relay)
+    def _():
+        for k in range(direct):
+            relay(k).wait_send()
+
+    left(0)
+    other_side(left)
 
     @pl.when(c > 0)
     def _():
@@ -437,6 +525,8 @@
             @pl.when(has_next)
             def _():
                 onward(step, k).wait_send()
+                if k < relayed:
+                    gather[step].beyond(k).wait_send()
 
 
 def on_device(groups, peers, fine_tiles, fine_cols, agg_of, prolong, coarse_cols):
@@ -446,7 +536,8 @@
     ints = jnp.concatenate([agg_of, coarse_cols.reshape(-1), fine_cols.reshape(-1)])
     room = -(-ints.shape[0] // 128) * 128
     ints = jnp.pad(ints, (0, room - ints.shape[0])).reshape(1, room)
-    share = rows // peers
+    assert groups % 2 == 0 and groups >= 4
+    direct = rows // (2 * peers) + rows // 4
     dma = pltpu.SemaphoreType.DMA
     tile = (width, width)
     packed = (width + width // 2, 2 * width // 3)
@@ -461,6 +552,7 @@
         scratch_shapes=[
             pltpu.VMEM((rows,) + tile, BF),
             pltpu.VMEM((rows,) + tile, BF),
+            pltpu.VMEM((rows,) + tile, BF),
             pltpu.VMEM((3 * rows,) + packed, BF),
             pltpu.VMEM((rows,) + tile, F32),
             pltpu.VMEM((slots * crows,) + packed, BF),
@@ -472,11 +564,11 @@
             pltpu.SMEM((rows,), jnp.int32),
             pltpu.SMEM((2 * rows,), jnp.int32),
             pltpu.SMEM((4 * crows * slots + crows,), jnp.int32),
-            dma((peers + 1,)), dma((3,)), dma((2,)), dma((2,)),
-            dma((2, 4, share)), dma((2, 4, share)),
+            dma((7,)), dma((3,)), dma((2,)), dma((2,)),
+            dma((2, 4, direct)), dma((2, 4, direct)),
             dma((slots, crows)), dma((slots, crows)),
-            dma((2, 4, crows)), dma((2, 4, crows)),
-            dma((2, 4, crows)), dma((2, 4, crows)),
+            dma((2, 5, crows)), dma((2, 5, crows)),
+            dma((2, 5, crows)), dma((2, 5, crows)),
         ],
         compiler_params=pltpu.CompilerParams(
             collective_id=0, has_side_effects=True, vmem_limit_bytes=56 * 1024 * 1024

time: 82.8 us -> 72.6 us (0.88); the launches traced: 82.6 us -> 71.5 us
  Pallas kernels: 76.9 us -> 65.8 us
    pallas_call x1, Pallas kernels: 76.9 us -> 65.8 us  [on_device(): pl.pallas_call(functools.partial(kernel, (groups, peers, rows, crows, slo...]
where the time goes in v1:
time: 72.6 us; the launch traced here: 71.5 us
  Pallas kernels  65.8 us (91%)
  local copies, waits for them, and re-layouts  4.3 us (6%)
  other arithmetic  0.75 us (1%)
    pallas_call x1, Pallas kernels, on_device(): pl.pallas_call(functools.partial(kernel, (groups, peers, rows, crows, slo...  65.8 us
    unnamed x4, local copies, waits for them, and re-layouts  3.02 us

profile of v1, /device:TPU:29, one launch (start us, length us, event | category | flops | bytes accessed | tf_op | source)
XLA Modules:
  0.0 71.5 jit_solution(4298422215634774002)
XLA Ops:
  0.6 0.8 %reshape.16 = s32[16]{0:T(128)S(1)} reshape(s32[4,4]{1,0:T(4,128)} %param.9) | data formatting | bytes 128 | tf_op jit(solution)/shard_map/reshape | solution.py:536
  1.4 0.7 %pad_add_fusion = s32[48]{0:T(128)S(1)} fusion(s32[16]{0:T(128)} %bitcast.5, s32[16]{0:T(128)S(1)} %reshape.16, s32[16]{0:T(128)} %param.7), kind=kLoop, calls=%fused_computation | loop fusion | flops 96 | bytes 384 | tf_op jit(solution)/shard_map/concatenate | solution.py:536
  2.1 0.5 pad_bitcast_fusion.ints
  2.7 65.8 %shard_map.68 = (f32[4,1,192,192]{3,2,1,0:T(8,128)}, f32[4,1,192,192]{3,2,1,0:T(8,128)}) custom-call(s32[1,128]{1,0:T(1,128)} %pad_bitcast_fusion.ints, bf16[16,192,192]{2,1,0:T(8,128)(2,1)} %bitcast.4, bf16[16,192,192]{2,1,0:T(8,128)(2,1)} %prolong_hbm.1), custom_call_target="tpu_custom_call" | custom-call | tf_op jit(solution)/shard_map/pallas_call | solution.py:547
  68.4 0.0 copy-start
  68.4 2.1 %copy.9 = f32[4,1,192,192]{3,2,1,0:T(8,128)} copy(f32[4,1,192,192]{3,2,1,0:T(8,128)} %get-tuple-element.4) | data formatting | bytes 1179648
  70.6 0.0 copy-done
  70.6 0.9 %copy.10 = f32[4,1,192,192]{3,2,1,0:T(8,128)} copy(f32[4,1,192,192]{3,2,1,0:T(8,128)S(1)} %copy-done) | data formatting | bytes 1179648
Async XLA Ops:
  68.4 2.1 %copy-start = (f32[4,1,192,192]{3,2,1,0:T(8,128)S(1)}, f32[4,1,192,192]{3,2,1,0:T(8,128)}, u32[]{:S(2)}) copy-start(f32[4,1,192,192]{3,2,1,0:T(8,128)} %get-tuple-element.5) | copy-start | bytes 1769476

commit v2 on v1

--- a/solution.py
+++ b/solution.py
@@ -196,9 +196,9 @@
         def _():
             act(ints_to(0, (a - 1, c)))
 
+    ints_all(lambda copy: copy.start())
     for k in range(direct):
         push(k).start()
-    ints_all(lambda copy: copy.start())
     for j in range(2, len(blocks)):
         take(j).wait()
         pack_own(j)
@@ -258,12 +258,12 @@
             arrived(0, k)
         if k >= lag:
             other_side(arrived, k - lag)
-
-    def turn(i, carry):
-        turned[i] = own_prolong[i].astype(F32).T.astype(BF)
-        return carry
-
-    lax.fori_loop(0, rows, turn, 0)
+        for i in range(k * rows // (direct + lag), (k + 1) * rows // (direct + lag)):
+            turned[i] = own_prolong[i].astype(F32).T.astype(BF)
+        if 0 <= k - 3 < alone:
+            crossed(0, k - 3)
+        if 0 <= k - 5 < alone:
+            other_side(crossed, k - 5)
     own_ints.wait()
 
     @pl.when(has_prev)
@@ -357,9 +357,9 @@
 
     lax.fori_loop(0, crows, ties, 0)
 
-    for k in range(alone):
+    for k in range(max(direct + lag - 3, 0), alone):
         crossed(0, k)
-    for k in range(alone):
+    for k in range(max(direct + lag - 5, 0), alone):
         other_side(crossed, k)
     take_fine.wait()
     complete(0)

time: 72.6 us -> 68.7 us (0.946)
  Pallas kernels: 65.8 us -> 62 us
    pallas_call x1, Pallas kernels: 65.8 us -> 62 us  [on_device(): pl.pallas_call(functools.partial(kernel, (groups, peers, rows, crows, slo...]
where the time goes in v2:
time: 68.7 us; the launch traced here: 67.7 us
  Pallas kernels  62 us (90%)
  local copies, waits for them, and re-layouts  4.3 us (6%)
  other arithmetic  0.75 us (1%)
    pallas_call x1, Pallas kernels, on_device(): pl.pallas_call(functools.partial(kernel, (groups, peers, rows, crows, slo...  62 us
    unnamed x4, local copies, waits for them, and re-layouts  3.02 us

profile of v2, /device:TPU:29, one launch (start us, length us, event | category | flops | bytes accessed | tf_op | source)
XLA Modules:
  0.0 67.7 jit_solution(11374336646470094710)
XLA Ops:
  0.6 0.8 %reshape.16 = s32[16]{0:T(128)S(1)} reshape(s32[4,4]{1,0:T(4,128)} %param.9) | data formatting | bytes 128 | tf_op jit(solution)/shard_map/reshape | solution.py:536
  1.4 0.7 %pad_add_fusion = s32[48]{0:T(128)S(1)} fusion(s32[16]{0:T(128)} %bitcast.5, s32[16]{0:T(128)S(1)} %reshape.16, s32[16]{0:T(128)} %param.7), kind=kLoop, calls=%fused_computation | loop fusion | flops 96 | bytes 384 | tf_op jit(solution)/shard_map/concatenate | solution.py:536
  2.1 0.5 pad_bitcast_fusion.ints
  2.7 62.0 %shard_map.68 = (f32[4,1,192,192]{3,2,1,0:T(8,128)}, f32[4,1,192,192]{3,2,1,0:T(8,128)}) custom-call(s32[1,128]{1,0:T(1,128)} %pad_bitcast_fusion.ints, bf16[16,192,192]{2,1,0:T(8,128)(2,1)} %bitcast.4, bf16[16,192,192]{2,1,0:T(8,128)(2,1)} %prolong_hbm.1), custom_call_target="tpu_custom_call" | custom-call | tf_op jit(solution)/shard_map/pallas_call | solution.py:547
  64.7 0.0 copy-start
  64.7 2.1 %copy.9 = f32[4,1,192,192]{3,2,1,0:T(8,128)} copy(f32[4,1,192,192]{3,2,1,0:T(8,128)} %get-tuple-element.4) | data formatting | bytes 1179648
  66.8 0.0 copy-done
  66.8 0.9 %copy.10 = f32[4,1,192,192]{3,2,1,0:T(8,128)} copy(f32[4,1,192,192]{3,2,1,0:T(8,128)S(1)} %copy-done) | data formatting | bytes 1179648
Async XLA Ops:
  64.7 2.1 %copy-start = (f32[4,1,192,192]{3,2,1,0:T(8,128)S(1)}, f32[4,1,192,192]{3,2,1,0:T(8,128)}, u32[]{:S(2)}) copy-start(f32[4,1,192,192]{3,2,1,0:T(8,128)} %get-tuple-element.5) | copy-start | bytes 1769476
